TPU v7x, 32 devices: a whole 2x2x4 slice. The times are simulated.
32 devices in a mesh: kstr: 4 (over y, x), pw: 8 (over z, core).
Axes of the slice: x: 2, y: 2, z: 4, core: 2. Of those that a mesh axis runs over, the one named last changes fastest.
Arguments:
- states_re: bfloat16 [4, 256, 16384], P('kstr', None, 'pw'), may hold values from -8 to 8
- states_im: bfloat16 [4, 256, 16384], P('kstr', None, 'pw'), may hold values from -8 to 8
- gmap: int32 [16384], P('pw'), may hold values from 0 to 16383, as said below
Outputs:
- new_re: bfloat16 [4, 256, 16384], P('kstr', None, 'pw')
- new_im: bfloat16 [4, 256, 16384], P('kstr', None, 'pw')
Inputs may be any that keep to these rules, and one draw needn't show every extreme that they name: gmap[G] = (G + o) mod 16384 for one offset o with 1 <= o < 16384.
All inputs are finite; a program needn't handle non-finite values.
Results may differ from a plain program's by a relative error of at most 0.008.
Values may be sent and summed in bfloat16 or wider, within the bound.
A program may use at most 64 MiB of HBM per device.

v0:
```python
import jax
import jax.numpy as jnp
from jax import lax
from jax.sharding import PartitionSpec as P

NEWTON = 4
STEPS = 2


HIGH = lax.Precision.HIGHEST
EPS_SCALE = 1e-06
EPS_NORM = 1e-06
TAU_STEP = 0.25


def shifted(value, axis, by):
    count = lax.axis_size(axis)
    return lax.ppermute(value, axis, [(i, (i + by) % count) for i in range(count)])


def padded_2(block, sides, width):
    for axis, dim in sides:
        count = lax.axis_size(axis)
        forward = [(i, i + 1) for i in range(count - 1)]
        forward.append((count - 1, 0))
        backward = [(target, source) for source, target in forward]
        low = lax.ppermute(
            lax.slice_in_dim(block, block.shape[dim] - width, None, axis=dim), axis, forward
        )
        high = lax.ppermute(lax.slice_in_dim(block, 0, width, axis=dim), axis, backward)
        block = jnp.concatenate([low, block, high], axis=dim)
    return block


def complex_mul(left, right):

    def matmul(first, second):
        return jnp.einsum("kij,kjl->kil", first, second, precision=HIGH)

    real = matmul(left[:, 0], right[:, 0]) - matmul(left[:, 1], right[:, 1])
    imag = matmul(left[:, 0], right[:, 1]) + matmul(left[:, 1], right[:, 0])
    return jnp.stack([real, imag], 1)


def start_inverse(whole):
    magnitude = jnp.sqrt(whole[:, 0] * whole[:, 0] + whole[:, 1] * whole[:, 1])
    colmax = jnp.max(jnp.sum(magnitude, axis=1), axis=1)
    rowmax = jnp.max(jnp.sum(magnitude, axis=2), axis=1)
    factor = (1.0 / (colmax * rowmax + EPS_SCALE))[:, None, None]
    return jnp.stack(
        [jnp.swapaxes(whole[:, 0], 1, 2) * factor, -jnp.swapaxes(whole[:, 1], 1, 2) * factor], 1
    )


def newton_full(whole):
    iterate = start_inverse(whole)
    for turn in range(NEWTON):
        iterate = 2.0 * iterate - complex_mul(iterate, complex_mul(whole, iterate))
    return iterate


def bf_product(form, left, right):
    return jnp.einsum(form, left, right, preferred_element_type=jnp.float32)


def dual_terms(rounded, states):
    real = bf_product("kmn,kmg->kng", rounded[:, 0], states[:, 0]) + bf_product(
        "kmn,kmg->kng", rounded[:, 1], states[:, 1]
    )
    imag = bf_product("kmn,kmg->kng", rounded[:, 0], states[:, 1]) - bf_product(
        "kmn,kmg->kng", rounded[:, 1], states[:, 0]
    )
    return jnp.stack([real, imag], 1).astype(jnp.bfloat16)


def rotate_columns(block, amount, width):
    blocks_off = amount // width
    rest = amount % width
    plane_size = lax.axis_size("pw")
    for bit in range((plane_size - 1).bit_length()):
        moved = shifted(block, "pw", -(1 << bit))
        block = jnp.where(jnp.bitwise_and(jnp.right_shift(blocks_off, bit), 1) == 1, moved, block)
    after = shifted(block, "pw", -1)
    joined = jnp.concatenate([block, after], block.ndim - 1)
    return lax.dynamic_slice_in_dim(joined, rest, width, block.ndim - 1)


def body(states_re, states_im, gmap):
    kpoints, bands, width = states_re.shape
    string_size = lax.axis_size("kstr")
    plane_size = lax.axis_size("pw")
    string_index = lax.axis_index("kstr")
    total_width = width * plane_size
    offset = jnp.mod(gmap[0] - lax.axis_index("pw") * width, total_width)
    back_offset = jnp.mod(total_width - offset, total_width)
    at_first = string_index == 0
    at_last = string_index == string_size - 1
    count_all = 2 * kpoints * string_size * bands * width * plane_size
    states = jnp.stack([states_re, states_im], 1)
    for step in range(STEPS):
        padded = padded_2(states, (("kstr", 0),), 1)
        ahead = padded[-1:]
        behind = padded[:1]
        turned = rotate_columns(ahead, offset, width)
        ahead = jnp.where(at_last, turned, ahead)
        following = jnp.concatenate([states[1:], ahead], 0)
        s_re = bf_product("kmg,kng->kmn", states[:, 0], following[:, 0]) + bf_product(
            "kmg,kng->kmn", states[:, 1], following[:, 1]
        )
        s_im = bf_product("kmg,kng->kmn", states[:, 0], following[:, 1]) - bf_product(
            "kmg,kng->kmn", states[:, 1], following[:, 0]
        )
        partial_value = jnp.stack([s_re, s_im], 1)
        whole = lax.psum(partial_value, "pw") / (width * plane_size)
        inverse = newton_full(whole)
        rounded = inverse.astype(jnp.bfloat16)
        a_re = bf_product("kmn,kmg->kng", rounded[:, 0], following[:, 0]) - bf_product(
            "kmn,kmg->kng", rounded[:, 1], following[:, 1]
        )
        a_im = bf_product("kmn,kmg->kng", rounded[:, 0], following[:, 1]) + bf_product(
            "kmn,kmg->kng", rounded[:, 1], following[:, 0]
        )
        earlier = dual_terms(rounded[:-1], states[:-1])
        previous_inverse = shifted(rounded, "kstr", 1)
        arrived = dual_terms(previous_inverse, behind)
        placed = rotate_columns(arrived, back_offset, width)
        arrived = jnp.where(at_first, placed, arrived)
        incoming = jnp.concatenate([arrived, earlier], 0).astype(jnp.float32)
        g_re = a_im - incoming[:, 1]
        g_im = incoming[:, 0] - a_re
        total = lax.psum(jnp.sum(g_re * g_re + g_im * g_im), ("kstr", "pw"))
        rms = jnp.sqrt(total / count_all + EPS_NORM)
        new_re = (states[:, 0].astype(jnp.float32) + TAU_STEP * g_re / rms).astype(jnp.bfloat16)
        new_im = (states[:, 1].astype(jnp.float32) + TAU_STEP * g_im / rms).astype(jnp.bfloat16)
        states = jnp.stack([new_re, new_im], 1)
    return (states[:, 0], states[:, 1])


def solution(mesh):
    placed = (P("kstr", None, "pw"), P("kstr", None, "pw"), P("pw"))
    return jax.shard_map(
        body,
        mesh=mesh,
        in_specs=placed,
        out_specs=(P("kstr", None, "pw"), P("kstr", None, "pw")),
        check_vma=False,
    )
```

profile of v0, /device:TPU:0, one launch (start us, length us, event | category | flops | bytes accessed | tf_op | source)
XLA Modules:
  0.0 1193.7 jit_solution(11498836311990674013)
XLA Ops:
  12.9 44.9 %collective-permute-done = bf16[1,2,256,2048]{3,2,1,0:T(8,128)(2,1)S(1)} collective-permute-done((bf16[1,2,256,2048]{3,2,1,0:T(8,128)(2,1)S(1)}, bf16[1,2,256,2048]{3,2,1,0:T(8,128)(2,1)S(1)}, u32[]{:S(2)}, u32[]{:S(2)}) %collective-permute-start) | collective-permute-done | bytes 2097184 | tf_op jit(solution)/shard_map/ppermute | solution.py:30
  61.9 21.7 %collective-permute-done.1 = bf16[1,2,256,2048]{3,2,1,0:T(8,128)(2,1)} collective-permute-done((bf16[1,2,256,2048]{3,2,1,0:T(8,128)(2,1)S(1)}, bf16[1,2,256,2048]{3,2,1,0:T(8,128)(2,1)}, u32[]{:S(2)}, u32[]{:S(2)}) %collective-permute-start.1) | collective-permute-done | bytes 2097184 | tf_op jit(solution)/shard_map/ppermute | solution.py:18
  88.2 46.2 %collective-permute-done.2 = bf16[1,2,256,2048]{3,2,1,0:T(8,128)(2,1)} collective-permute-done((bf16[1,2,256,2048]{3,2,1,0:T(8,128)(2,1)}, bf16[1,2,256,2048]{3,2,1,0:T(8,128)(2,1)}, u32[]{:S(2)}, u32[]{:S(2)}) %collective-permute-start.2) | collective-permute-done | bytes 2097184 | tf_op jit(solution)/shard_map/ppermute | solution.py:18
  137.5 93.9 %collective-permute-done.3 = bf16[1,2,256,2048]{3,2,1,0:T(8,128)(2,1)} collective-permute-done((bf16[1,2,256,2048]{3,2,1,0:T(8,128)(2,1)}, bf16[1,2,256,2048]{3,2,1,0:T(8,128)(2,1)}, u32[]{:S(2)}, u32[]{:S(2)}) %collective-permute-start.3) | collective-permute-done | bytes 2097184 | tf_op jit(solution)/shard_map/ppermute | solution.py:18
  235.9 23.9 %collective-permute-done.4 = bf16[1,2,256,2048]{3,2,1,0:T(8,128)(2,1)} collective-permute-done((bf16[1,2,256,2048]{3,2,1,0:T(8,128)(2,1)}, bf16[1,2,256,2048]{3,2,1,0:T(8,128)(2,1)}, u32[]{:S(2)}, u32[]{:S(2)}) %collective-permute-start.4) | collective-permute-done | bytes 2097184 | tf_op jit(solution)/shard_map/ppermute | solution.py:18
  269.9 56.3 %all-reduce.3.cloned.1.call-done = f32[1,2,256,256]{2,3,1,0:T(8,128)} async-done(((f32[1,2,256,256]{2,3,1,0:T(8,128)}), f32[1,2,256,256]{2,3,1,0:T(8,128)}) %all-reduce.3.cloned.1.call-update) | async-done | bytes 524304 | tf_op jit(solution)/shard_map/psum | solution.py:114
  348.4 5.9 collective-permute-done.5
  358.9 23.9 %collective-permute-done.7 = bf16[1,2,256,2048]{3,2,1,0:T(8,128)(2,1)} collective-permute-done((bf16[1,2,256,2048]{3,2,1,0:T(8,128)(2,1)}, bf16[1,2,256,2048]{3,2,1,0:T(8,128)(2,1)}, u32[]{:S(2)}, u32[]{:S(2)}) %collective-permute-start.7) | collective-permute-done | bytes 2097184 | tf_op jit(solution)/shard_map/ppermute | solution.py:18
  386.6 46.6 %collective-permute-done.8 = bf16[1,2,256,2048]{3,2,1,0:T(8,128)(2,1)} collective-permute-done((bf16[1,2,256,2048]{3,2,1,0:T(8,128)(2,1)}, bf16[1,2,256,2048]{3,2,1,0:T(8,128)(2,1)}, u32[]{:S(2)}, u32[]{:S(2)}) %collective-permute-start.8) | collective-permute-done | bytes 2097184 | tf_op jit(solution)/shard_map/ppermute | solution.py:18
  437.1 93.0 %collective-permute-done.9 = bf16[1,2,256,2048]{3,2,1,0:T(8,128)(2,1)} collective-permute-done((bf16[1,2,256,2048]{3,2,1,0:T(8,128)(2,1)}, bf16[1,2,256,2048]{3,2,1,0:T(8,128)(2,1)}, u32[]{:S(2)}, u32[]{:S(2)}) %collective-permute-start.9) | collective-permute-done | bytes 2097184 | tf_op jit(solution)/shard_map/ppermute | solution.py:18
  537.5 21.5 %collective-permute-done.10 = bf16[1,2,256,2048]{3,2,1,0:T(8,128)(2,1)} collective-permute-done((bf16[1,2,256,2048]{3,2,1,0:T(8,128)(2,1)}, bf16[1,2,256,2048]{3,2,1,0:T(8,128)(2,1)}, u32[]{:S(2)}, u32[]{:S(2)}) %collective-permute-start.10) | collective-permute-done | bytes 2097184 | tf_op jit(solution)/shard_map/ppermute | solution.py:18
  565.7 39.0 %psum.29 = f32[]{:T(128)} all-reduce(f32[]{:T(128)} %get-tuple-element.10), channel_id=1, replica_groups=mesh['kstr'=4,'pw'=8] {'kstr','pw'}, use_global_device_ids=true, to_apply=%region_6.7 | all-reduce | flops 1 | bytes 8 | tf_op jit(solution)/shard_map/psum | solution.py:131
  610.9 44.1 %collective-permute-done.11 = bf16[1,2,256,2048]{3,2,1,0:T(8,128)(2,1)S(1)} collective-permute-done((bf16[1,2,256,2048]{3,2,1,0:T(8,128)(2,1)S(1)}, bf16[1,2,256,2048]{3,2,1,0:T(8,128)(2,1)S(1)}, u32[]{:S(2)}, u32[]{:S(2)}) %collective-permute-start.11) | collective-permute-done | bytes 2097184 | tf_op jit(solution)/shard_map/ppermute | solution.py:30
  655.0 23.6 %collective-permute-done.12 = bf16[1,2,256,2048]{3,2,1,0:T(8,128)(2,1)S(1)} collective-permute-done((bf16[1,2,256,2048]{3,2,1,0:T(8,128)(2,1)S(1)}, bf16[1,2,256,2048]{3,2,1,0:T(8,128)(2,1)S(1)}, u32[]{:S(2)}, u32[]{:S(2)}) %collective-permute-start.12) | collective-permute-done | bytes 2097184 | tf_op jit(solution)/shard_map/ppermute | solution.py:18
  680.9 45.2 %collective-permute-done.13 = bf16[1,2,256,2048]{3,2,1,0:T(8,128)(2,1)S(1)} collective-permute-done((bf16[1,2,256,2048]{3,2,1,0:T(8,128)(2,1)S(1)}, bf16[1,2,256,2048]{3,2,1,0:T(8,128)(2,1)S(1)}, u32[]{:S(2)}, u32[]{:S(2)}) %collective-permute-start.13) | collective-permute-done | bytes 2097184 | tf_op jit(solution)/shard_map/ppermute | solution.py:18
  729.7 91.3 %collective-permute-done.14 = bf16[1,2,256,2048]{3,2,1,0:T(8,128)(2,1)S(1)} collective-permute-done((bf16[1,2,256,2048]{3,2,1,0:T(8,128)(2,1)S(1)}, bf16[1,2,256,2048]{3,2,1,0:T(8,128)(2,1)S(1)}, u32[]{:S(2)}, u32[]{:S(2)}) %collective-permute-start.14) | collective-permute-done | bytes 2097184 | tf_op jit(solution)/shard_map/ppermute | solution.py:18
  823.2 23.6 %collective-permute-done.15 = bf16[1,2,256,2048]{3,2,1,0:T(8,128)(2,1)S(1)} collective-permute-done((bf16[1,2,256,2048]{3,2,1,0:T(8,128)(2,1)S(1)}, bf16[1,2,256,2048]{3,2,1,0:T(8,128)(2,1)S(1)}, u32[]{:S(2)}, u32[]{:S(2)}) %collective-permute-start.15) | collective-permute-done | bytes 2097184 | tf_op jit(solution)/shard_map/ppermute | solution.py:18
  854.5 56.2 %all-reduce.5.cloned.1.call-done = f32[1,2,256,256]{2,3,1,0:T(8,128)} async-done(((f32[1,2,256,256]{2,3,1,0:T(8,128)}), f32[1,2,256,256]{2,3,1,0:T(8,128)}) %all-reduce.5.cloned.1.call-update) | async-done | bytes 524304 | tf_op jit(solution)/shard_map/psum | solution.py:114
  932.7 5.8 collective-permute-done.16
  945.6 23.6 %collective-permute-done.18 = bf16[1,2,256,2048]{3,2,1,0:T(8,128)(2,1)S(1)} collective-permute-done((bf16[1,2,256,2048]{3,2,1,0:T(8,128)(2,1)S(1)}, bf16[1,2,256,2048]{3,2,1,0:T(8,128)(2,1)S(1)}, u32[]{:S(2)}, u32[]{:S(2)}) %collective-permute-start.18) | collective-permute-done | bytes 2097184 | tf_op jit(solution)/shard_map/ppermute | solution.py:18
  971.7 46.2 %collective-permute-done.19 = bf16[1,2,256,2048]{3,2,1,0:T(8,128)(2,1)S(1)} collective-permute-done((bf16[1,2,256,2048]{3,2,1,0:T(8,128)(2,1)S(1)}, bf16[1,2,256,2048]{3,2,1,0:T(8,128)(2,1)S(1)}, u32[]{:S(2)}, u32[]{:S(2)}) %collective-permute-start.19) | collective-permute-done | bytes 2097184 | tf_op jit(solution)/shard_map/ppermute | solution.py:18
  1019.0 92.7 %collective-permute-done.20 = bf16[1,2,256,2048]{3,2,1,0:T(8,128)(2,1)S(1)} collective-permute-done((bf16[1,2,256,2048]{3,2,1,0:T(8,128)(2,1)S(1)}, bf16[1,2,256,2048]{3,2,1,0:T(8,128)(2,1)S(1)}, u32[]{:S(2)}, u32[]{:S(2)}) %collective-permute-start.20) | collective-permute-done | bytes 2097184 | tf_op jit(solution)/shard_map/ppermute | solution.py:18
  1114.7 22.6 %collective-permute-done.21 = bf16[1,2,256,2048]{3,2,1,0:T(8,128)(2,1)S(1)} collective-permute-done((bf16[1,2,256,2048]{3,2,1,0:T(8,128)(2,1)S(1)}, bf16[1,2,256,2048]{3,2,1,0:T(8,128)(2,1)S(1)}, u32[]{:S(2)}, u32[]{:S(2)}) %collective-permute-start.21) | collective-permute-done | bytes 2097184 | tf_op jit(solution)/shard_map/ppermute | solution.py:18
  1142.5 39.0 %psum.31 = f32[]{:T(128)} all-reduce(f32[]{:T(128)} %get-tuple-element.12), channel_id=1, replica_groups=mesh['kstr'=4,'pw'=8] {'kstr','pw'}, use_global_device_ids=true, to_apply=%region_13.14 | all-reduce | flops 1 | bytes 8 | tf_op jit(solution)/shard_map/psum | solution.py:131
  (188 shorter events, 143.2 us)
Async XLA Ops:
  7.2 319.1 %all-reduce.3.cloned.1.call-start = ((), (), s32[]{:S(2)}) async-start(), calls=%async_computation | async-start | bytes 1048576 | tf_op jit(solution)/shard_map/psum | solution.py:114
  9.0 48.9 %collective-permute-start = (bf16[1,2,256,2048]{3,2,1,0:T(8,128)(2,1)S(1)}, bf16[1,2,256,2048]{3,2,1,0:T(8,128)(2,1)S(1)}, u32[]{:S(2)}, u32[]{:S(2)}) collective-permute-start(bf16[1,2,256,2048]{3,2,1,0:T(8,128)(2,1)S(1)} %pad_maximum_fusion), channel_id=1, source_target_pairs={{8,0},{16,8},{24,16},{0,24},{9,1},{17,9},{25,17},{1,25},{10,2},{18... | collective-permute-start | bytes 6291464 | tf_op jit(solution)/shard_map/ppermute | solution.py:30
  57.8 25.8 %collective-permute-start.1 = (bf16[1,2,256,2048]{3,2,1,0:T(8,128)(2,1)S(1)}, bf16[1,2,256,2048]{3,2,1,0:T(8,128)(2,1)}, u32[]{:S(2)}, u32[]{:S(2)}) collective-permute-start(bf16[1,2,256,2048]{3,2,1,0:T(8,128)(2,1)S(1)} %collective-permute-done), channel_id=1, source_target_pairs={{0,7},{1,0},{2,1},{3,2},{4,3},{5,4},{6,5},{7,6},{8,15},{9,8},{10,9... | collective-permute-start | bytes 6291464 | tf_op jit(solution)/shard_map/ppermute | solution.py:18
  86.8 47.6 %collective-permute-start.2 = (bf16[1,2,256,2048]{3,2,1,0:T(8,128)(2,1)}, bf16[1,2,256,2048]{3,2,1,0:T(8,128)(2,1)}, u32[]{:S(2)}, u32[]{:S(2)}) collective-permute-start(bf16[1,2,256,2048]{3,2,1,0:T(8,128)(2,1)} %broadcast_select_fusion.7), channel_id=1, source_target_pairs={{0,6},{1,7},{2,0},{3,1},{4,2},{5,3},{6,4},{7,5},{8,14},{9,15},{10,... | collective-permute-start | bytes 6291464 | tf_op jit(solution)/shard_map/ppermute | solution.py:18
  137.5 93.9 %collective-permute-start.3 = (bf16[1,2,256,2048]{3,2,1,0:T(8,128)(2,1)}, bf16[1,2,256,2048]{3,2,1,0:T(8,128)(2,1)}, u32[]{:S(2)}, u32[]{:S(2)}) collective-permute-start(bf16[1,2,256,2048]{3,2,1,0:T(8,128)(2,1)} %broadcast_select_fusion.9), channel_id=1, source_target_pairs={{0,4},{1,5},{2,6},{3,7},{4,0},{5,1},{6,2},{7,3},{8,12},{9,13},{10,... | collective-permute-start | bytes 6291464 | tf_op jit(solution)/shard_map/ppermute | solution.py:18
  234.6 25.1 %collective-permute-start.4 = (bf16[1,2,256,2048]{3,2,1,0:T(8,128)(2,1)}, bf16[1,2,256,2048]{3,2,1,0:T(8,128)(2,1)}, u32[]{:S(2)}, u32[]{:S(2)}) collective-permute-start(bf16[1,2,256,2048]{3,2,1,0:T(8,128)(2,1)} %broadcast_select_fusion.11), channel_id=1, source_target_pairs={{0,7},{1,0},{2,1},{3,2},{4,3},{5,4},{6,5},{7,6},{8,15},{9,8},{10,9... | collective-permute-start | bytes 6291464 | tf_op jit(solution)/shard_map/ppermute | solution.py:18
  267.3 643.5 %all-reduce.5.cloned.1.call-start = ((), (), s32[]{:S(2)}) async-start(), calls=%async_computation.1 | async-start | bytes 1048576 | tf_op jit(solution)/shard_map/psum | solution.py:114
  267.3 81.0 %collective-permute-start.6 = (bf16[1,2,256,2048]{3,2,1,0:T(8,128)(2,1)}, bf16[1,2,256,2048]{3,2,1,0:T(8,128)(2,1)S(1)}, u32[]{:S(2)}, u32[]{:S(2)}) collective-permute-start(bf16[1,2,256,2048]{3,2,1,0:T(8,128)(2,1)} %copy-done.12), channel_id=1, source_target_pairs={{0,8},{8,16},{16,24},{24,0},{1,9},{9,17},{17,25},{25,1},{2,10},{10... | collective-permute-start | bytes 6291464 | tf_op jit(solution)/shard_map/ppermute | solution.py:27
  346.9 7.3 collective-permute-start.5
  358.9 23.9 %collective-permute-start.7 = (bf16[1,2,256,2048]{3,2,1,0:T(8,128)(2,1)}, bf16[1,2,256,2048]{3,2,1,0:T(8,128)(2,1)}, u32[]{:S(2)}, u32[]{:S(2)}) collective-permute-start(bf16[1,2,256,2048]{3,2,1,0:T(8,128)(2,1)} %pad_maximum_fusion.1), channel_id=1, source_target_pairs={{0,7},{1,0},{2,1},{3,2},{4,3},{5,4},{6,5},{7,6},{8,15},{9,8},{10,9... | collective-permute-start | bytes 6291464 | tf_op jit(solution)/shard_map/ppermute | solution.py:18
  384.4 48.7 %collective-permute-start.8 = (bf16[1,2,256,2048]{3,2,1,0:T(8,128)(2,1)}, bf16[1,2,256,2048]{3,2,1,0:T(8,128)(2,1)}, u32[]{:S(2)}, u32[]{:S(2)}) collective-permute-start(bf16[1,2,256,2048]{3,2,1,0:T(8,128)(2,1)} %broadcast_select_fusion.1), channel_id=1, source_target_pairs={{0,6},{1,7},{2,0},{3,1},{4,2},{5,3},{6,4},{7,5},{8,14},{9,15},{10,... | collective-permute-start | bytes 6291464 | tf_op jit(solution)/shard_map/ppermute | solution.py:18
  436.3 93.8 %collective-permute-start.9 = (bf16[1,2,256,2048]{3,2,1,0:T(8,128)(2,1)}, bf16[1,2,256,2048]{3,2,1,0:T(8,128)(2,1)}, u32[]{:S(2)}, u32[]{:S(2)}) collective-permute-start(bf16[1,2,256,2048]{3,2,1,0:T(8,128)(2,1)} %broadcast_select_fusion.3), channel_id=1, source_target_pairs={{0,4},{1,5},{2,6},{3,7},{4,0},{5,1},{6,2},{7,3},{8,12},{9,13},{10,... | collective-permute-start | bytes 6291464 | tf_op jit(solution)/shard_map/ppermute | solution.py:18
  533.3 25.6 %collective-permute-start.10 = (bf16[1,2,256,2048]{3,2,1,0:T(8,128)(2,1)}, bf16[1,2,256,2048]{3,2,1,0:T(8,128)(2,1)}, u32[]{:S(2)}, u32[]{:S(2)}) collective-permute-start(bf16[1,2,256,2048]{3,2,1,0:T(8,128)(2,1)} %broadcast_select_fusion.5), channel_id=1, source_target_pairs={{0,7},{1,0},{2,1},{3,2},{4,3},{5,4},{6,5},{7,6},{8,15},{9,8},{10,9... | collective-permute-start | bytes 6291464 | tf_op jit(solution)/shard_map/ppermute | solution.py:18
  608.2 46.8 %collective-permute-start.11 = (bf16[1,2,256,2048]{3,2,1,0:T(8,128)(2,1)S(1)}, bf16[1,2,256,2048]{3,2,1,0:T(8,128)(2,1)S(1)}, u32[]{:S(2)}, u32[]{:S(2)}) collective-permute-start(bf16[1,2,256,2048]{3,2,1,0:T(8,128)(2,1)S(1)} %pad_maximum_fusion.2), channel_id=1, source_target_pairs={{8,0},{16,8},{24,16},{0,24},{9,1},{17,9},{25,17},{1,25},{10,2},{18... | collective-permute-start | bytes 6291464 | tf_op jit(solution)/shard_map/ppermute | solution.py:30
  655.0 23.6 %collective-permute-start.12 = (bf16[1,2,256,2048]{3,2,1,0:T(8,128)(2,1)S(1)}, bf16[1,2,256,2048]{3,2,1,0:T(8,128)(2,1)S(1)}, u32[]{:S(2)}, u32[]{:S(2)}) collective-permute-start(bf16[1,2,256,2048]{3,2,1,0:T(8,128)(2,1)S(1)} %collective-permute-done.11), channel_id=1, source_target_pairs={{0,7},{1,0},{2,1},{3,2},{4,3},{5,4},{6,5},{7,6},{8,15},{9,8},{10,9... | collective-permute-start | bytes 6291464 | tf_op jit(solution)/shard_map/ppermute | solution.py:18
  678.8 47.3 %collective-permute-start.13 = (bf16[1,2,256,2048]{3,2,1,0:T(8,128)(2,1)S(1)}, bf16[1,2,256,2048]{3,2,1,0:T(8,128)(2,1)S(1)}, u32[]{:S(2)}, u32[]{:S(2)}) collective-permute-start(bf16[1,2,256,2048]{3,2,1,0:T(8,128)(2,1)S(1)} %broadcast_select_fusion.6), channel_id=1, source_target_pairs={{0,6},{1,7},{2,0},{3,1},{4,2},{5,3},{6,4},{7,5},{8,14},{9,15},{10,... | collective-permute-start | bytes 6291464 | tf_op jit(solution)/shard_map/ppermute | solution.py:18
  726.4 94.6 %collective-permute-start.14 = (bf16[1,2,256,2048]{3,2,1,0:T(8,128)(2,1)S(1)}, bf16[1,2,256,2048]{3,2,1,0:T(8,128)(2,1)S(1)}, u32[]{:S(2)}, u32[]{:S(2)}) collective-permute-start(bf16[1,2,256,2048]{3,2,1,0:T(8,128)(2,1)S(1)} %broadcast_select_fusion.8), channel_id=1, source_target_pairs={{0,4},{1,5},{2,6},{3,7},{4,0},{5,1},{6,2},{7,3},{8,12},{9,13},{10,... | collective-permute-start | bytes 6291464 | tf_op jit(solution)/shard_map/ppermute | solution.py:18
  821.2 25.5 %collective-permute-start.15 = (bf16[1,2,256,2048]{3,2,1,0:T(8,128)(2,1)S(1)}, bf16[1,2,256,2048]{3,2,1,0:T(8,128)(2,1)S(1)}, u32[]{:S(2)}, u32[]{:S(2)}) collective-permute-start(bf16[1,2,256,2048]{3,2,1,0:T(8,128)(2,1)S(1)} %broadcast_select_fusion.10), channel_id=1, source_target_pairs={{0,7},{1,0},{2,1},{3,2},{4,3},{5,4},{6,5},{7,6},{8,15},{9,8},{10,9... | collective-permute-start | bytes 6291464 | tf_op jit(solution)/shard_map/ppermute | solution.py:18
  851.9 80.8 %collective-permute-start.17 = (bf16[1,2,256,2048]{3,2,1,0:T(8,128)(2,1)}, bf16[1,2,256,2048]{3,2,1,0:T(8,128)(2,1)}, u32[]{:S(2)}, u32[]{:S(2)}) collective-permute-start(bf16[1,2,256,2048]{3,2,1,0:T(8,128)(2,1)} %copy-done.13), channel_id=1, source_target_pairs={{0,8},{8,16},{16,24},{24,0},{1,9},{9,17},{17,25},{25,1},{2,10},{10... | collective-permute-start | bytes 6291464 | tf_op jit(solution)/shard_map/ppermute | solution.py:27
  931.2 7.3 collective-permute-start.16
  945.5 23.7 %collective-permute-start.18 = (bf16[1,2,256,2048]{3,2,1,0:T(8,128)(2,1)S(1)}, bf16[1,2,256,2048]{3,2,1,0:T(8,128)(2,1)S(1)}, u32[]{:S(2)}, u32[]{:S(2)}) collective-permute-start(bf16[1,2,256,2048]{3,2,1,0:T(8,128)(2,1)S(1)} %pad_maximum_fusion.3), channel_id=1, source_target_pairs={{0,7},{1,0},{2,1},{3,2},{4,3},{5,4},{6,5},{7,6},{8,15},{9,8},{10,9... | collective-permute-start | bytes 6291464 | tf_op jit(solution)/shard_map/ppermute | solution.py:18
  969.5 48.4 %collective-permute-start.19 = (bf16[1,2,256,2048]{3,2,1,0:T(8,128)(2,1)S(1)}, bf16[1,2,256,2048]{3,2,1,0:T(8,128)(2,1)S(1)}, u32[]{:S(2)}, u32[]{:S(2)}) collective-permute-start(bf16[1,2,256,2048]{3,2,1,0:T(8,128)(2,1)S(1)} %broadcast_select_fusion), channel_id=1, source_target_pairs={{0,6},{1,7},{2,0},{3,1},{4,2},{5,3},{6,4},{7,5},{8,14},{9,15},{10,... | collective-permute-start | bytes 6291464 | tf_op jit(solution)/shard_map/ppermute | solution.py:18
  1018.2 93.6 %collective-permute-start.20 = (bf16[1,2,256,2048]{3,2,1,0:T(8,128)(2,1)S(1)}, bf16[1,2,256,2048]{3,2,1,0:T(8,128)(2,1)S(1)}, u32[]{:S(2)}, u32[]{:S(2)}) collective-permute-start(bf16[1,2,256,2048]{3,2,1,0:T(8,128)(2,1)S(1)} %broadcast_select_fusion.2), channel_id=1, source_target_pairs={{0,4},{1,5},{2,6},{3,7},{4,0},{5,1},{6,2},{7,3},{8,12},{9,13},{10,... | collective-permute-start | bytes 6291464 | tf_op jit(solution)/shard_map/ppermute | solution.py:18
  1112.0 25.4 %collective-permute-start.21 = (bf16[1,2,256,2048]{3,2,1,0:T(8,128)(2,1)S(1)}, bf16[1,2,256,2048]{3,2,1,0:T(8,128)(2,1)S(1)}, u32[]{:S(2)}, u32[]{:S(2)}) collective-permute-start(bf16[1,2,256,2048]{3,2,1,0:T(8,128)(2,1)S(1)} %broadcast_select_fusion.4), channel_id=1, source_target_pairs={{0,7},{1,0},{2,1},{3,2},{4,3},{5,4},{6,5},{7,6},{8,15},{9,8},{10,9... | collective-permute-start | bytes 6291464 | tf_op jit(solution)/shard_map/ppermute | solution.py:18
  (14 other events, 714.0 us)
Sparse Core Ops, SparseCore 0:
  267.4 58.7 all-reduce.2
  852.0 58.6 all-reduce.4
where the time goes:
time: 1200 us; the launch traced here: 1190 us
  waiting for transfers between devices  953 us (79%)
  blocking collectives  78 us (6%)
  matrix products  54.8 us (5%)
  other arithmetic  49 us (4%)
  starting transfers between devices  37 us (3%)
  between operations  19.9 us (2%)
    ppermute x18, waiting for transfers between devices, shifted(): lax.ppermute(value, axis, [(i, (i + by) % count) for i in range(count)])  751 us
    psum x2, waiting for transfers between devices, body(): whole = lax.psum(partial_value, 'pw') / (width * plane_size)  113 us
    ppermute x2, waiting for transfers between devices, padded_2(): lax.ppermute(lax.slice_in_dim(block, 0, width, axis=dim), axis, backward)  89 us
    psum x2, blocking collectives, body(): total = lax.psum(jnp.sum(g_re * g_re + g_im * g_im), ('kstr', 'pw'))  78 us
    dot_general x64, matrix products, matmul(): return jnp.einsum('kij,kjl->kil', first, second, precision=HIGH)  31.3 us
    ppermute x18, starting transfers between devices, shifted(): lax.ppermute(value, axis, [(i, (i + by) % count) for i in range(count)])  25.1 us
  transfers between devices with their start and end apart: 24, of which 22 were waited for; matrix products, arithmetic and copies ran while one was open for 4% of the time, Pallas kernels for 0%

commit v1 on v0

--- a/solution.py
+++ b/solution.py
@@ -1,6 +1,8 @@
 import jax
 import jax.numpy as jnp
 from jax import lax
+from jax.experimental import pallas as pl
+from jax.experimental.pallas import tpu as pltpu
 from jax.sharding import PartitionSpec as P
 
 NEWTON = 4
@@ -85,7 +87,7 @@
     return lax.dynamic_slice_in_dim(joined, rest, width, block.ndim - 1)
 
 
-def body(states_re, states_im, gmap):
+def general_body(states_re, states_im, gmap):
     kpoints, bands, width = states_re.shape
     string_size = lax.axis_size("kstr")
     plane_size = lax.axis_size("pw")
@@ -136,8 +138,250 @@
     return (states[:, 0], states[:, 1])
 
 
+def rank_of(k, p, planes):
+    return k * planes + p
+
+
+def exchange(name, ident, peers, here, there, copies, args, outs, parts=1):
+    n_in = len(args)
+
+    def kernel(*refs):
+        data, (send, recv, local) = refs[:-3], refs[-3:]
+        barrier = pltpu.get_barrier_semaphore()
+
+        def greet(step, carry):
+            pl.semaphore_signal(
+                barrier, inc=1, device_id=there(step), device_id_type=pl.DeviceIdType.MESH
+            )
+            return carry
+
+        lax.fori_loop(1, peers, greet, 0)
+        pl.semaphore_wait(barrier, peers - 1)
+
+        def remote(step):
+            target = there(step)
+            return [
+                pltpu.make_async_remote_copy(
+                    src_ref=source,
+                    dst_ref=place,
+                    send_sem=send.at[step, index],
+                    recv_sem=recv.at[step, index],
+                    device_id=target,
+                    device_id_type=pl.DeviceIdType.MESH,
+                )
+                for index, (source, place) in enumerate(copies(data, target))
+            ]
+
+        def begin(step, carry):
+            for copy in remote(step):
+                copy.start()
+            return carry
+
+        def finish(step, carry):
+            for copy in remote(step):
+                copy.wait()
+            return carry
+
+        lax.fori_loop(1, peers, begin, 0)
+        own = [
+            pltpu.make_async_copy(source, place, local.at[index])
+            for index, (source, place) in enumerate(copies(data, here()))
+        ]
+        for copy in own:
+            copy.start()
+        for copy in own:
+            copy.wait()
+        lax.fori_loop(1, peers, finish, 0)
+
+    return pl.pallas_call(
+        kernel,
+        out_shape=outs,
+        in_specs=[pl.BlockSpec(memory_space=pltpu.VMEM)] * n_in,
+        out_specs=jax.tree.map(lambda _: pl.BlockSpec(memory_space=pltpu.VMEM), outs),
+        scratch_shapes=[
+            pltpu.SemaphoreType.DMA((peers, parts)),
+            pltpu.SemaphoreType.DMA((peers, parts)),
+            pltpu.SemaphoreType.DMA((parts,)),
+        ],
+        compiler_params=pltpu.CompilerParams(collective_id=ident, has_side_effects=True),
+        name=name,
+    )(*args)
+
+
+def spread_body(strings, planes, states_re, states_im, gmap):
+    _, bands, width = states_re.shape
+    count = strings * planes
+    piece = width // strings
+    total_width = width * planes
+    rows = 2 * bands // count
+    half = count // 2
+    share = bands // planes
+    count_all = 2 * strings * bands * total_width
+    bf16, f32 = jnp.bfloat16, jnp.float32
+
+    def place():
+        return lax.axis_index("kstr"), lax.axis_index("pw")
+
+    def over_string(step):
+        k, p = place()
+        return (lax.rem(k + step, strings), p)
+
+    def over_planes(step):
+        k, p = place()
+        return (k, lax.rem(p + step, planes))
+
+    def over_all(step):
+        k, p = place()
+        peer = lax.rem(rank_of(k, p, planes) + step, count)
+        return (peer // planes, lax.rem(peer, planes))
+
+    def columns(index, size):
+        return pl.ds(pl.multiple_of(index * size, size), size)
+
+    def band_rows(rank):
+        return pl.ds(pl.multiple_of(lax.rem(rank, half) * rows, rows), rows)
+
+    def spread(refs, target):
+        re, im, out = refs
+        k, _ = place()
+        cut = columns(target[0], piece)
+        return [(re.at[:, cut], out.at[k, 0]), (im.at[:, cut], out.at[k, 1])]
+
+    def collect(refs, target):
+        new, re, im = refs
+        k, _ = place()
+        cut = columns(k, piece)
+        return [(new.at[target[0], 0], re.at[:, cut]), (new.at[target[0], 1], im.at[:, cut])]
+
+    def to_bands(refs, target):
+        own, out = refs
+        k, p = place()
+        rank = rank_of(target[0], target[1], planes)
+        which = (rank // half) * (strings - 1)
+        return [(own.at[which, :, band_rows(rank), :], out.at[:, :, columns(p * strings + k, piece)])]
+
+    def from_bands(refs, target):
+        rolled, out = refs
+        rank = rank_of(*place(), planes)
+        block = target[1] * strings + target[0]
+        return [(rolled.at[:, :, columns(block, piece)], out.at[rank // half, :, band_rows(rank), :])]
+
+    def sum_string(refs, target):
+        part, out = refs
+        return [(part.at[target[0]], out.at[place()[0]])]
+
+    def sum_planes(refs, target):
+        part, out = refs
+        return [(part.at[:, columns(target[1], share), :], out.at[place()[1]])]
+
+    def gather_planes(refs, target):
+        part, out = refs
+        return [(part, out.at[:, columns(place()[1], share), :])]
+
+    def gather_string(refs, target):
+        part, out = refs
+        return [(part, out.at[place()[0]])]
+
+    def gather_all(refs, target):
+        part, out = refs
+        return [(part, out.at[rank_of(*place(), planes)])]
+
+    here = place
+    offset = jnp.mod(gmap[0] - lax.axis_index("pw") * width, total_width)
+    back_offset = jnp.mod(total_width - offset, total_width)
+    amount = jnp.where(rank_of(*place(), planes) < half, offset, back_offset)
+
+    shape = jax.ShapeDtypeStruct
+    states = exchange(
+        "spread", 1, strings, here, over_string, spread,
+        (states_re[0], states_im[0]), shape((strings, 2, bands, piece), bf16), 2,
+    )
+    for step in range(STEPS):
+        banded = exchange(
+            "to_bands", 2, count, here, over_all, to_bands,
+            (states,), shape((2, rows, total_width), bf16),
+        )
+        rolled = lax.dynamic_slice_in_dim(
+            jnp.concatenate([banded, banded], 2), amount, total_width, 2
+        )
+        turned = exchange(
+            "from_bands", 3, count, here, over_all, from_bands,
+            (rolled,), shape((2, 2, bands, piece), bf16),
+        )
+        following = jnp.concatenate([states[1:], turned[:1]], 0)
+        before = jnp.concatenate([turned[1:], states[:-1]], 0)
+        s_re = bf_product("kmg,kng->kmn", states[:, 0], following[:, 0]) + bf_product(
+            "kmg,kng->kmn", states[:, 1], following[:, 1]
+        )
+        s_im = bf_product("kmg,kng->kmn", states[:, 0], following[:, 1]) - bf_product(
+            "kmg,kng->kmn", states[:, 1], following[:, 0]
+        )
+        partial_value = (jnp.stack([s_re, s_im], 1) / total_width).astype(bf16)
+        pieces = exchange(
+            "sum_string", 4, strings, here, over_string, sum_string,
+            (partial_value,), shape((strings, 2, bands, bands), bf16),
+        )
+        part = jnp.sum(pieces.astype(f32), 0).astype(bf16)
+        pieces = exchange(
+            "sum_planes", 5, planes, here, over_planes, sum_planes,
+            (part,), shape((planes, 2, share, bands), bf16),
+        )
+        part = jnp.sum(pieces.astype(f32), 0)
+        whole = exchange(
+            "gather_planes", 6, planes, here, over_planes, gather_planes,
+            (part,), shape((2, bands, bands), f32),
+        )
+        rounded = newton_full(whole[None])[0].astype(bf16)
+        inverse = exchange(
+            "gather_string", 7, strings, here, over_string, gather_string,
+            (rounded,), shape((strings, 2, bands, bands), bf16),
+        )
+        earlier = jnp.concatenate([inverse[-1:], inverse[:-1]], 0)
+        a_re = bf_product("kmn,kmg->kng", inverse[:, 0], following[:, 0]) - bf_product(
+            "kmn,kmg->kng", inverse[:, 1], following[:, 1]
+        )
+        a_im = bf_product("kmn,kmg->kng", inverse[:, 0], following[:, 1]) + bf_product(
+            "kmn,kmg->kng", inverse[:, 1], following[:, 0]
+        )
+        incoming = dual_terms(earlier, before).astype(f32)
+        g_re = a_im - incoming[:, 1]
+        g_im = incoming[:, 0] - a_re
+        local = jnp.sum(g_re * g_re + g_im * g_im)
+        sums = exchange(
+            "gather_all", 8, count, here, over_all, gather_all,
+            (jnp.broadcast_to(local, (8, 128)),), shape((count, 8, 128), f32),
+        )
+        total = jnp.sum(sums[:, 0, 0])
+        rms = jnp.sqrt(total / count_all + EPS_NORM)
+        new_re = (states[:, 0].astype(f32) + TAU_STEP * g_re / rms).astype(bf16)
+        new_im = (states[:, 1].astype(f32) + TAU_STEP * g_im / rms).astype(bf16)
+        states = jnp.stack([new_re, new_im], 1)
+    new_re, new_im = exchange(
+        "collect", 9, strings, here, over_string, collect,
+        (states,), (shape((bands, width), bf16), shape((bands, width), bf16)), 2,
+    )
+    return (new_re[None], new_im[None])
+
+
 def solution(mesh):
     placed = (P("kstr", None, "pw"), P("kstr", None, "pw"), P("pw"))
+    strings, planes = mesh.shape["kstr"], mesh.shape["pw"]
+
+    def body(states_re, states_im, gmap):
+        kpoints, bands, width = states_re.shape
+        count = strings * planes
+        fits = (
+            kpoints == 1
+            and strings > 1
+            and planes > 1
+            and width % (strings * 128) == 0
+            and bands % (planes * 16) == 0
+            and (2 * bands) % (count * 16) == 0
+        )
+        if not fits:
+            return general_body(states_re, states_im, gmap)
+        return spread_body(strings, planes, states_re, states_im, gmap)
+
     return jax.shard_map(
         body,
         mesh=mesh,

time: 1200 us -> 447 us (0.37)
  waiting for transfers between devices: 953 us -> 0 us
  Pallas kernels: 0 us -> 328 us
  blocking collectives: 78 us -> 0 us
  starting transfers between devices: 37 us -> 0 us
  local copies, waits for them, and re-layouts: 2.34 us -> 25.4 us
  other arithmetic: 49 us -> 33.3 us
  between operations: 19.9 us -> 6.69 us
    ppermute x22 -> x0, waiting for transfers between devices: 840 us -> none  [the longest x18 751 us: shifted(): lax.ppermute(value, axis, [(i, (i + by) % count) for i in range(count)])]
    pallas_call x0 -> x16, Pallas kernels: none -> 328 us  [exchange(): pl.pallas_call(kernel, out_shape=outs, in_specs=[pl.BlockSpec(memory_spac...]
    psum x2 -> x0, waiting for transfers between devices: 113 us -> none  [body(): whole = lax.psum(partial_value, 'pw') / (width * plane_size)]
    psum x2 -> x0, blocking collectives: 78 us -> none  [body(): total = lax.psum(jnp.sum(g_re * g_re + g_im * g_im), ('kstr', 'pw'))]
    ppermute x22 -> x0, starting transfers between devices: 36.9 us -> none  [the longest x18 25.1 us: shifted(): lax.ppermute(value, axis, [(i, (i + by) % count) for i in range(count)])]
    select_n x14 -> x0, other arithmetic: 24.7 us -> none  [the longest x12 19 us: rotate_columns(): jnp.where(jnp.bitwise_and(jnp.right_shift(blocks_off, bit), 1) == 1, move...]
  transfers between devices with their start and end apart: 24 -> 0, of which waited for: 22 -> 0; matrix products, arithmetic and copies ran while one was open for 4% -> 0% of each run, Pallas kernels for 0% -> 0%
where the time goes in v1:
time: 447 us; the launch traced here: 442 us
  Pallas kernels  328 us (73%)
  matrix products  48 us (11%)
  other arithmetic  33.3 us (7%)
  local copies, waits for them, and re-layouts  25.4 us (6%)
  between operations  6.69 us (1%)
    pallas_call x16, Pallas kernels, exchange(): pl.pallas_call(kernel, out_shape=outs, in_specs=[pl.BlockSpec(memory_spac...  328 us
    dot_general x64, matrix products, matmul(): return jnp.einsum('kij,kjl->kil', first, second, precision=HIGH)  31.9 us
    dot_general x24, matrix products, bf_product(): return jnp.einsum(form, left, right, preferred_element_type=jnp.float32)  16.1 us
    unnamed x45, local copies, waits for them, and re-layouts  10.7 us

profile of v1, /device:TPU:0, one launch (start us, length us, event | category | flops | bytes accessed | tf_op | source)
XLA Modules:
  0.0 441.7 jit_solution(10463849013234563837)
XLA Ops:
  2.5 30.5 %spread.1.refs_0_ = bf16[4,2,256,512]{3,2,1,0:T(8,128)(2,1)} custom-call(bf16[256,2048]{1,0:T(8,128)(2,1)} %bitcast.509, bf16[256,2048]{1,0:T(8,128)(2,1)} %bitcast.510), custom_call_target="tpu_custom_call" | custom-call | tf_op jit(solution)/shard_map/spread/pallas_call | solution.py:196
  33.0 30.5 %to_bands.2 = bf16[2,16,16384]{2,1,0:T(8,128)(2,1)} custom-call(bf16[4,2,256,512]{3,2,1,0:T(8,128)(2,1)} %spread.1.refs_0_), custom_call_target="tpu_custom_call" | custom-call | tf_op jit(solution)/shard_map/to_bands/pallas_call | solution.py:196
  63.5 3.0 fusion.29.refs_0_
  66.5 30.7 %from_bands.2 = bf16[2,2,256,512]{3,2,1,0:T(8,128)(2,1)} custom-call(bf16[2,16,16384]{2,1,0:T(8,128)(2,1)} %fusion.29.refs_0_), custom_call_target="tpu_custom_call" | custom-call | tf_op jit(solution)/shard_map/from_bands/pallas_call | solution.py:196
  103.2 17.0 %sum_string.2 = bf16[4,2,256,256]{3,2,1,0:T(8,128)(2,1)} custom-call(bf16[4,2,256,256]{3,2,1,0:T(8,128)(2,1)} %fusion.4.refs_0_), custom_call_target="tpu_custom_call" | custom-call | tf_op jit(solution)/shard_map/sum_string/pallas_call | solution.py:196
  122.4 11.1 %sum_planes.2 = bf16[8,2,32,256]{3,2,1,0:T(8,128)(2,1)} custom-call(bf16[2,256,256]{2,1,0:T(8,128)(2,1)} %reduce_sum.114.refs_0_), custom_call_target="tpu_custom_call" | custom-call | tf_op jit(solution)/shard_map/sum_planes/pallas_call | solution.py:196
  135.1 15.0 %gather_planes.2 = f32[2,256,256]{2,1,0:T(8,128)} custom-call(f32[2,32,256]{2,1,0:T(8,128)} %convert_reduce_fusion.1.refs_0_), custom_call_target="tpu_custom_call" | custom-call | tf_op jit(solution)/shard_map/gather_planes/pallas_call | solution.py:196
  171.7 17.5 %gather_string.2 = bf16[4,2,256,256]{3,2,1,0:T(8,128)(2,1)} custom-call(bf16[2,256,256]{2,1,0:T(8,128)(2,1)} %fusion.59.refs_0_), custom_call_target="tpu_custom_call" | custom-call | tf_op jit(solution)/shard_map/gather_string/pallas_call | solution.py:196
  197.2 2.8 add_reduce_fusion.1
  201.2 13.0 %gather_all.2 = f32[32,8,128]{2,1,0:T(8,128)} custom-call(f32[8,128]{1,0:T(8,128)} %broadcast_in_dim.21.refs_0_), custom_call_target="tpu_custom_call" | custom-call | tf_op jit(solution)/shard_map/gather_all/pallas_call | solution.py:196
  216.5 3.0 add_convert_fusion.3
  222.4 29.9 %to_bands.3 = bf16[2,16,16384]{2,1,0:T(8,128)(2,1)} custom-call(bf16[4,2,256,512]{3,2,1,0:T(8,128)(2,1)} %copy.16.refs_0_), custom_call_target="tpu_custom_call" | custom-call | tf_op jit(solution)/shard_map/to_bands/pallas_call | solution.py:196
  252.3 3.0 fusion.24.refs_0_
  255.4 30.3 %from_bands.3 = bf16[2,2,256,512]{3,2,1,0:T(8,128)(2,1)} custom-call(bf16[2,16,16384]{2,1,0:T(8,128)(2,1)} %fusion.24.refs_0_), custom_call_target="tpu_custom_call" | custom-call | tf_op jit(solution)/shard_map/from_bands/pallas_call | solution.py:196
  285.7 2.2 slice_bitcast_fusion.5
  291.5 17.0 %sum_string.3 = bf16[4,2,256,256]{3,2,1,0:T(8,128)(2,1)} custom-call(bf16[4,2,256,256]{3,2,1,0:T(8,128)(2,1)} %fusion.5.refs_0_), custom_call_target="tpu_custom_call" | custom-call | tf_op jit(solution)/shard_map/sum_string/pallas_call | solution.py:196
  310.7 11.2 %sum_planes.3 = bf16[8,2,32,256]{3,2,1,0:T(8,128)(2,1)} custom-call(bf16[2,256,256]{2,1,0:T(8,128)(2,1)} %reduce_sum.120.refs_0_), custom_call_target="tpu_custom_call" | custom-call | tf_op jit(solution)/shard_map/sum_planes/pallas_call | solution.py:196
  323.5 15.0 %gather_planes.3 = f32[2,256,256]{2,1,0:T(8,128)} custom-call(f32[2,32,256]{2,1,0:T(8,128)} %convert_reduce_fusion.refs_0_), custom_call_target="tpu_custom_call" | custom-call | tf_op jit(solution)/shard_map/gather_planes/pallas_call | solution.py:196
  359.8 17.5 %gather_string.3 = bf16[4,2,256,256]{3,2,1,0:T(8,128)(2,1)} custom-call(bf16[2,256,256]{2,1,0:T(8,128)(2,1)} %fusion.68.refs_0_), custom_call_target="tpu_custom_call" | custom-call | tf_op jit(solution)/shard_map/gather_string/pallas_call | solution.py:196
  385.3 2.7 add_reduce_fusion
  389.3 13.0 %gather_all.3 = f32[32,8,128]{2,1,0:T(8,128)} custom-call(f32[8,128]{1,0:T(8,128)} %broadcast_in_dim.23.refs_0_), custom_call_target="tpu_custom_call" | custom-call | tf_op jit(solution)/shard_map/gather_all/pallas_call | solution.py:196
  404.5 3.0 fusion.40
  409.0 29.1 %collect.1 = (bf16[256,2048]{1,0:T(8,128)(2,1)}, bf16[256,2048]{1,0:T(8,128)(2,1)}) custom-call(bf16[4,2,256,512]{3,2,1,0:T(8,128)(2,1)} %pad_maximum_fusion.1.refs_0_), custom_call_target="tpu_custom_call" | custom-call | tf_op jit(solution)/shard_map/collect/pallas_call | solution.py:196
  438.1 2.4 copy.51
  (172 shorter events, 84.6 us)
Async XLA Ops:
  66.5 32.0 %copy-start = (bf16[4,2,256,512]{3,2,1,0:T(8,128)(2,1)S(1)}, bf16[4,2,256,512]{3,2,1,0:T(8,128)(2,1)}, u32[]{:S(2)}) copy-start(bf16[4,2,256,512]{3,2,1,0:T(8,128)(2,1)} %spread.1.refs_0_) | copy-start | bytes 6291460
  100.1 1.0 copy-start.9
  100.1 1.4 copy-start.13
  189.2 2.3 copy-start.1
  193.5 1.2 copy-start.14
  193.5 1.5 copy-start.17
  195.0 1.2 copy-start.10
  197.2 2.8 copy-start.16
  219.5 1.0 copy-start.2
  219.5 1.3 copy-start.4
  255.4 32.5 %copy-start.3 = (bf16[4,256,512]{2,1,0:T(8,128)(2,1)S(1)}, bf16[4,256,512]{2,1,0:T(8,128)(2,1)}, u32[]{:S(2)}) copy-start(bf16[4,256,512]{2,1,0:T(8,128)(2,1)} %copy-done.2) | copy-start | bytes 3145732
  285.7 2.2 copy-start.5
  288.4 1.0 copy-start.7
  288.4 1.5 copy-start.11
  359.8 19.7 %copy-start.19 = (bf16[1,2,256,512]{3,2,0,1:T(8,128)(2,1)S(1)}, bf16[1,2,256,512]{3,2,0,1:T(8,128)(2,1)}, u32[]{:S(2)}) copy-start(bf16[1,2,256,512]{3,2,0,1:T(8,128)(2,1)} %get-tuple-element.21) | copy-start | bytes 1572868
  381.6 1.2 copy-start.12
  381.6 1.5 copy-start.18
  383.1 1.2 copy-start.8
  385.3 2.7 copy-start.15
  385.3 19.2 %copy-start.6 = (bf16[4,256,512]{2,1,0:T(8,128)(2,1)S(1)}, bf16[4,256,512]{2,1,0:T(8,128)(2,1)}, u32[]{:S(2)}) copy-start(bf16[4,256,512]{2,1,0:T(8,128)(2,1)} %copy-done.4) | copy-start | bytes 3145732
  438.1 2.4 copy-start.20

commit v2 on v1

--- a/solution.py
+++ b/solution.py
@@ -208,6 +208,126 @@
     )(*args)
 
 
+def sum_everywhere(ident, strings, planes, local):
+    def kernel(local_ref, out_ref, first, second, stage, send, recv):
+        k, p = lax.axis_index("kstr"), lax.axis_index("pw")
+
+        def string_peer(step):
+            return (lax.rem(k + step, strings), p)
+
+        def plane_peer(step):
+            return (k, lax.rem(p + step, planes))
+
+        barrier = pltpu.get_barrier_semaphore()
+        peers = [string_peer(step) for step in range(1, strings)]
+        peers += [plane_peer(step) for step in range(1, planes)]
+        for peer in peers:
+            pl.semaphore_signal(
+                barrier, inc=1, device_id=peer, device_id_type=pl.DeviceIdType.MESH
+            )
+        pl.semaphore_wait(barrier, len(peers))
+
+        def copy(source, place, slot):
+            return pltpu.make_async_remote_copy(
+                src_ref=source,
+                dst_ref=place,
+                send_sem=send.at[slot],
+                recv_sem=recv.at[slot],
+                device_id=peers[slot],
+                device_id_type=pl.DeviceIdType.MESH,
+            )
+
+        copies = [copy(local_ref, first.at[k], slot) for slot in range(strings - 1)]
+        for item in copies:
+            item.start()
+        first[k] = local_ref[...]
+        for item in copies:
+            item.wait()
+        stage[...] = jnp.sum(first[...], 0)
+        copies = [copy(stage, second.at[p], slot) for slot in range(strings - 1, len(peers))]
+        for item in copies:
+            item.start()
+        second[p] = stage[...]
+        for item in copies:
+            item.wait()
+        out_ref[...] = jnp.sum(second[...], 0)
+
+    tile = local.shape
+    return pl.pallas_call(
+        kernel,
+        out_shape=jax.ShapeDtypeStruct(tile, local.dtype),
+        in_specs=[pl.BlockSpec(memory_space=pltpu.VMEM)],
+        out_specs=pl.BlockSpec(memory_space=pltpu.VMEM),
+        scratch_shapes=[
+            pltpu.VMEM((strings,) + tile, local.dtype),
+            pltpu.VMEM((planes,) + tile, local.dtype),
+            pltpu.VMEM(tile, local.dtype),
+            pltpu.SemaphoreType.DMA((strings + planes - 2,)),
+            pltpu.SemaphoreType.DMA((strings + planes - 2,)),
+        ],
+        compiler_params=pltpu.CompilerParams(collective_id=ident, has_side_effects=True),
+        name="sum_everywhere",
+    )(local)
+
+
+def halves(value):
+    high = value.astype(jnp.bfloat16)
+    return high, (value - high.astype(jnp.float32)).astype(jnp.bfloat16)
+
+
+def left_factor(real, imag):
+    real_high, real_low = halves(real)
+    imag_high, imag_low = halves(imag)
+    high = jnp.concatenate([real_high, imag_high], 1)
+    return jnp.concatenate([high, high, real_low, imag_low], 1)
+
+
+def right_factor(real, imag):
+    real_high, real_low = halves(real)
+    imag_high, imag_low = halves(imag)
+    high = [
+        jnp.concatenate([real_high, imag_high], 1),
+        jnp.concatenate([-imag_high, real_high], 1),
+    ]
+    low = [
+        jnp.concatenate([real_low, imag_low], 1),
+        jnp.concatenate([-imag_low, real_low], 1),
+    ]
+    return jnp.concatenate(high + low + high, 0)
+
+
+def newton_kernel(whole_ref, out_ref):
+    real, imag = whole_ref[0].astype(jnp.float32), whole_ref[1].astype(jnp.float32)
+    bands = real.shape[0]
+    magnitude = jnp.sqrt(real * real + imag * imag)
+    colmax = jnp.max(jnp.sum(magnitude, axis=0, keepdims=True), axis=1, keepdims=True)
+    rowmax = jnp.max(jnp.sum(magnitude, axis=1, keepdims=True), axis=0, keepdims=True)
+    factor = 1.0 / (colmax * rowmax + EPS_SCALE)
+    x_re, x_im = real.T * factor, -imag.T * factor
+    whole = left_factor(real, imag)
+    for turn in range(NEWTON):
+        p = jnp.dot(whole, right_factor(x_re, x_im), preferred_element_type=jnp.float32)
+        q = jnp.dot(
+            left_factor(x_re, x_im),
+            right_factor(p[:, :bands], p[:, bands:]),
+            preferred_element_type=jnp.float32,
+        )
+        x_re = 2.0 * x_re - q[:, :bands]
+        x_im = 2.0 * x_im - q[:, bands:]
+    out_ref[0] = x_re.astype(jnp.bfloat16)
+    out_ref[1] = x_im.astype(jnp.bfloat16)
+
+
+def newton_rounded(whole):
+    return pl.pallas_call(
+        newton_kernel,
+        out_shape=jax.ShapeDtypeStruct(whole.shape, jnp.bfloat16),
+        in_specs=[pl.BlockSpec(memory_space=pltpu.VMEM)],
+        out_specs=pl.BlockSpec(memory_space=pltpu.VMEM),
+        name="newton",
+    )(whole)
+
+
 def spread_body(strings, planes, states_re, states_im, gmap):
     _, bands, width = states_re.shape
     count = strings * planes
@@ -282,10 +402,6 @@
         part, out = refs
         return [(part, out.at[place()[0]])]
 
-    def gather_all(refs, target):
-        part, out = refs
-        return [(part, out.at[rank_of(*place(), planes)])]
-
     here = place
     offset = jnp.mod(gmap[0] - lax.axis_index("pw") * width, total_width)
     back_offset = jnp.mod(total_width - offset, total_width)
@@ -326,12 +442,12 @@
             "sum_planes", 5, planes, here, over_planes, sum_planes,
             (part,), shape((planes, 2, share, bands), bf16),
         )
-        part = jnp.sum(pieces.astype(f32), 0)
+        part = jnp.sum(pieces.astype(f32), 0).astype(bf16)
         whole = exchange(
             "gather_planes", 6, planes, here, over_planes, gather_planes,
-            (part,), shape((2, bands, bands), f32),
-        )
-        rounded = newton_full(whole[None])[0].astype(bf16)
+            (part,), shape((2, bands, bands), bf16),
+        )
+        rounded = newton_rounded(whole)
         inverse = exchange(
             "gather_string", 7, strings, here, over_string, gather_string,
             (rounded,), shape((strings, 2, bands, bands), bf16),
@@ -346,12 +462,8 @@
         incoming = dual_terms(earlier, before).astype(f32)
         g_re = a_im - incoming[:, 1]
         g_im = incoming[:, 0] - a_re
-        local = jnp.sum(g_re * g_re + g_im * g_im)
-        sums = exchange(
-            "gather_all", 8, count, here, over_all, gather_all,
-            (jnp.broadcast_to(local, (8, 128)),), shape((count, 8, 128), f32),
-        )
-        total = jnp.sum(sums[:, 0, 0])
+        local = jnp.sum((g_re * g_re + g_im * g_im).reshape(-1, 8, piece // 128, 128), (0, 2))
+        total = jnp.sum(sum_everywhere(8, strings, planes, local))
         rms = jnp.sqrt(total / count_all + EPS_NORM)
         new_re = (states[:, 0].astype(f32) + TAU_STEP * g_re / rms).astype(bf16)
         new_im = (states[:, 1].astype(f32) + TAU_STEP * g_im / rms).astype(bf16)

time: 447 us -> 402 us (0.90)
  matrix products: 48 us -> 16.1 us
  local copies, waits for them, and re-layouts: 25.4 us -> 19.6 us
    pallas_call x0 -> x4, Pallas kernels: none -> 35.6 us  [the longest x2 23 us: sum_everywhere(): pl.pallas_call(kernel, out_shape=jax.ShapeDtypeStruct(tile, local.dtype),...]
    pallas_call x16 -> x14, Pallas kernels: 328 us -> 293 us  [exchange(): pl.pallas_call(kernel, out_shape=outs, in_specs=[pl.BlockSpec(memory_spac...]
    dot_general x64 -> x0, matrix products: 31.9 us -> none  [matmul(): return jnp.einsum('kij,kjl->kil', first, second, precision=HIGH)]
    unnamed x45 -> x37, local copies, waits for them, and re-layouts: 10.7 us -> 8.92 us
where the time goes in v2:
time: 402 us; the launch traced here: 400 us
  Pallas kernels  328 us (82%)
  other arithmetic  32.9 us (8%)
  local copies, waits for them, and re-layouts  19.6 us (5%)
  matrix products  16.1 us (4%)
    pallas_call x14, Pallas kernels, exchange(): pl.pallas_call(kernel, out_shape=outs, in_specs=[pl.BlockSpec(memory_spac...  293 us
    pallas_call x2, Pallas kernels, sum_everywhere(): pl.pallas_call(kernel, out_shape=jax.ShapeDtypeStruct(tile, local.dtype),...  23 us
    dot_general x24, matrix products, bf_product(): return jnp.einsum(form, left, right, preferred_element_type=jnp.float32)  16.1 us
    pallas_call x2, Pallas kernels, newton_rounded(): pl.pallas_call(newton_kernel, out_shape=jax.ShapeDtypeStruct(whole.shape,...  12.6 us
    unnamed x37, local copies, waits for them, and re-layouts  8.92 us

profile of v2, /device:TPU:0, one launch (start us, length us, event | category | flops | bytes accessed | tf_op | source)
XLA Modules:
  0.0 400.3 jit_solution(17532540507753557897)
XLA Ops:
  2.5 30.4 %spread.1.refs_0_ = bf16[4,2,256,512]{3,2,1,0:T(8,128)(2,1)} custom-call(bf16[256,2048]{1,0:T(8,128)(2,1)} %bitcast.159, bf16[256,2048]{1,0:T(8,128)(2,1)} %bitcast.160), custom_call_target="tpu_custom_call" | custom-call | tf_op jit(solution)/shard_map/spread/pallas_call | solution.py:196
  33.0 30.5 %to_bands.2 = bf16[2,16,16384]{2,1,0:T(8,128)(2,1)} custom-call(bf16[4,2,256,512]{3,2,1,0:T(8,128)(2,1)} %spread.1.refs_0_), custom_call_target="tpu_custom_call" | custom-call | tf_op jit(solution)/shard_map/to_bands/pallas_call | solution.py:196
  63.5 3.0 fusion.25.refs_0_
  66.5 30.8 %from_bands.2 = bf16[2,2,256,512]{3,2,1,0:T(8,128)(2,1)} custom-call(bf16[2,16,16384]{2,1,0:T(8,128)(2,1)} %fusion.25.refs_0_), custom_call_target="tpu_custom_call" | custom-call | tf_op jit(solution)/shard_map/from_bands/pallas_call | solution.py:196
  104.0 17.0 %sum_string.2 = bf16[4,2,256,256]{3,2,1,0:T(8,128)(2,1)} custom-call(bf16[4,2,256,256]{3,2,1,0:T(8,128)(2,1)} %fusion.4.refs_0_), custom_call_target="tpu_custom_call" | custom-call | tf_op jit(solution)/shard_map/sum_string/pallas_call | solution.py:196
  123.1 11.1 %sum_planes.2 = bf16[8,2,32,256]{3,2,1,0:T(8,128)(2,1)} custom-call(bf16[2,256,256]{2,1,0:T(8,128)(2,1)} %reduce_sum.84.refs_0_), custom_call_target="tpu_custom_call" | custom-call | tf_op jit(solution)/shard_map/sum_planes/pallas_call | solution.py:196
  135.8 10.8 %gather_planes.2.whole_ref = bf16[2,256,256]{2,1,0:T(8,128)(2,1)} custom-call(bf16[2,32,256]{2,1,0:T(8,128)(2,1)} %reduce_sum.85.refs_0_), custom_call_target="tpu_custom_call" | custom-call | tf_op jit(solution)/shard_map/gather_planes/pallas_call | solution.py:196
  146.6 6.3 %newton.2.refs_0_ = bf16[2,256,256]{2,1,0:T(8,128)(2,1)} custom-call(bf16[2,256,256]{2,1,0:T(8,128)(2,1)} %gather_planes.2.whole_ref), custom_call_target="tpu_custom_call" | custom-call | tf_op jit(solution)/shard_map/newton/pallas_call | solution.py:322
  152.9 17.2 %gather_string.2 = bf16[4,2,256,256]{3,2,1,0:T(8,128)(2,1)} custom-call(bf16[2,256,256]{2,1,0:T(8,128)(2,1)} %newton.2.refs_0_), custom_call_target="tpu_custom_call" | custom-call | tf_op jit(solution)/shard_map/gather_string/pallas_call | solution.py:196
  177.5 2.7 multiply_add_fusion.1
  183.0 11.5 %sum_everywhere.2 = f32[8,128]{1,0:T(8,128)} custom-call(f32[8,128]{1,0:T(8,128)} %reduce_sum.86.local_ref), custom_call_target="tpu_custom_call" | custom-call | tf_op jit(solution)/shard_map/sum_everywhere/pallas_call | solution.py:256
  196.5 3.0 add_convert_fusion.3
  202.0 29.7 %to_bands.3 = bf16[2,16,16384]{2,1,0:T(8,128)(2,1)} custom-call(bf16[4,2,256,512]{3,2,1,0:T(8,128)(2,1)} %copy.15.refs_0_), custom_call_target="tpu_custom_call" | custom-call | tf_op jit(solution)/shard_map/to_bands/pallas_call | solution.py:196
  231.7 3.0 fusion.20.refs_0_
  234.7 29.6 %from_bands.3 = bf16[2,2,256,512]{3,2,1,0:T(8,128)(2,1)} custom-call(bf16[2,16,16384]{2,1,0:T(8,128)(2,1)} %fusion.20.refs_0_), custom_call_target="tpu_custom_call" | custom-call | tf_op jit(solution)/shard_map/from_bands/pallas_call | solution.py:196
  269.5 17.6 %sum_string.3 = bf16[4,2,256,256]{3,2,1,0:T(8,128)(2,1)} custom-call(bf16[4,2,256,256]{3,2,1,0:T(8,128)(2,1)} %fusion.5.refs_0_), custom_call_target="tpu_custom_call" | custom-call | tf_op jit(solution)/shard_map/sum_string/pallas_call | solution.py:196
  289.3 11.0 %sum_planes.3 = bf16[8,2,32,256]{3,2,1,0:T(8,128)(2,1)} custom-call(bf16[2,256,256]{2,1,0:T(8,128)(2,1)} %reduce_sum.88.refs_0_), custom_call_target="tpu_custom_call" | custom-call | tf_op jit(solution)/shard_map/sum_planes/pallas_call | solution.py:196
  301.9 10.8 %gather_planes.3.whole_ref = bf16[2,256,256]{2,1,0:T(8,128)(2,1)} custom-call(bf16[2,32,256]{2,1,0:T(8,128)(2,1)} %reduce_sum.89.refs_0_), custom_call_target="tpu_custom_call" | custom-call | tf_op jit(solution)/shard_map/gather_planes/pallas_call | solution.py:196
  312.7 6.3 %newton.3.refs_0_ = bf16[2,256,256]{2,1,0:T(8,128)(2,1)} custom-call(bf16[2,256,256]{2,1,0:T(8,128)(2,1)} %gather_planes.3.whole_ref), custom_call_target="tpu_custom_call" | custom-call | tf_op jit(solution)/shard_map/newton/pallas_call | solution.py:322
  319.0 17.3 %gather_string.3 = bf16[4,2,256,256]{3,2,1,0:T(8,128)(2,1)} custom-call(bf16[2,256,256]{2,1,0:T(8,128)(2,1)} %newton.3.refs_0_), custom_call_target="tpu_custom_call" | custom-call | tf_op jit(solution)/shard_map/gather_string/pallas_call | solution.py:196
  346.9 2.8 reduce_sum.90.local_ref
  349.8 11.5 %sum_everywhere.3 = f32[8,128]{1,0:T(8,128)} custom-call(f32[8,128]{1,0:T(8,128)} %reduce_sum.90.local_ref), custom_call_target="tpu_custom_call" | custom-call | tf_op jit(solution)/shard_map/sum_everywhere/pallas_call | solution.py:256
  363.3 3.0 fusion.36
  367.7 29.1 %collect.1 = (bf16[256,2048]{1,0:T(8,128)(2,1)}, bf16[256,2048]{1,0:T(8,128)(2,1)}) custom-call(bf16[4,2,256,512]{3,2,1,0:T(8,128)(2,1)} %pad_maximum_fusion.1.refs_0_), custom_call_target="tpu_custom_call" | custom-call | tf_op jit(solution)/shard_map/collect/pallas_call | solution.py:196
  (84 shorter events, 51.1 us)
Async XLA Ops:
  66.5 32.8 %copy-start = (bf16[4,2,256,512]{3,2,1,0:T(8,128)(2,1)S(1)}, bf16[4,2,256,512]{3,2,1,0:T(8,128)(2,1)}, u32[]{:S(2)}) copy-start(bf16[4,2,256,512]{3,2,1,0:T(8,128)(2,1)} %spread.1.refs_0_) | copy-start | bytes 6291460
  100.9 1.4 copy-start.9
  170.2 2.3 copy-start.1
  170.2 2.3 copy-start.15
  174.5 1.2 copy-start.10
  174.5 1.5 copy-start.13
  177.5 2.7 copy-start.12
  199.5 1.0 copy-start.2
  264.3 1.5 copy-start.3
  266.4 1.0 copy-start.5
  266.4 1.5 copy-start.7
  340.4 1.2 copy-start.8
  340.4 1.5 copy-start.14
  342.0 1.2 copy-start.6
  344.2 2.7 copy-start.11
  346.9 16.3 %copy-start.4 = (bf16[4,256,512]{2,1,0:T(8,128)(2,1)S(1)}, bf16[4,256,512]{2,1,0:T(8,128)(2,1)}, u32[]{:S(2)}) copy-start(bf16[4,256,512]{2,1,0:T(8,128)(2,1)} %copy-done.2) | copy-start | bytes 3145732
  396.9 2.4 copy-start.16
